TPU v7x, 32 devices: a whole 2x2x4 slice. The times are simulated.
32 devices in a mesh: rep: 2 (over y), ctx: 4 (over z), head: 2 (over x), sub: 2 (over core).
Axes of the slice: x: 2, y: 2, z: 4, core: 2. Of those that a mesh axis runs over, the one named last changes fastest.
Arguments:
- hidden_states: bfloat16 [2048, 4096], P(('rep', 'ctx'), ('head', 'sub')), parts along dimension 0, may hold values from -8 to 8
- w_query: bfloat16 [4096, 2048], P('ctx', ('head', 'sub')), may hold values from -0.09375 to 0.09375
- w_key: bfloat16 [4096, 2048], P('ctx', ('head', 'sub')), may hold values from -0.09375 to 0.09375
- w_value: bfloat16 [4096, 2048], P('ctx', ('head', 'sub')), may hold values from -0.09375 to 0.09375
- a_query: bfloat16 [4096, 8], replicated, may hold values from -0.09375 to 0.09375
- a_value: bfloat16 [4096, 8], replicated, may hold values from -0.09375 to 0.09375
- b_query: bfloat16 [8, 2048], P(None, ('head', 'sub')), may hold values from -0.29882812 to 0.29882812
- b_value: bfloat16 [8, 2048], P(None, ('head', 'sub')), may hold values from -0.29882812 to 0.29882812
- positions: int32 [2048], P(('rep', 'ctx')), parts along dimension 0, may hold values from 0 to 99999, as said below
- out_grad: bfloat16 [2048, 2048], P(('rep', 'ctx'), ('head', 'sub')), parts along dimension 0, may hold values from -0.119628906 to 0.119628906
Outputs:
- attn_out: bfloat16 [2048, 2048], P(('rep', 'ctx'), ('head', 'sub')), parts along dimension 0
- grad_a_query: float32 [4096, 16], P(None, 'rep'), parts along dimension 1
- grad_b_query: float32 [16, 2048], P('rep', ('head', 'sub')), parts along dimension 0
- grad_a_value: float32 [4096, 16], P(None, 'rep'), parts along dimension 1
- grad_b_value: float32 [16, 2048], P('rep', ('head', 'sub')), parts along dimension 0
There are 2 independent parts, one for each index of `rep`. A program takes and returns all parts, laid end to end along the dimension named above; an argument that names none is the same for every part. Nothing has to cross between parts.
Inputs may be any that keep to these rules, and one draw needn't show every extreme that they name: `positions`: strictly increasing along the sequence; the first is 0 and the last is 99999.
All inputs are finite; a program needn't handle non-finite values.
Results may differ from a plain program's by a relative error of at most 0.012.
Values may be sent and summed in bfloat16 or wider, within the bound.
A program may use at most 64 MiB of HBM per device.

v0:
```python
import math
import jax
import jax.numpy as jnp
from jax import lax
from jax.sharding import PartitionSpec as P

HEAD_DIM = 128
HEADS = 16
TRAIN_CTX = 4096
MAX_POS = 100000


def passed_along(block, axis, distance):
    devices = range(lax.axis_size(axis))
    route = [((i - distance) % len(devices), i) for i in devices]
    return lax.ppermute(block, axis, route)


def rope_tables(positions):
    half_dim = HEAD_DIM // 2
    inverse = jnp.exp(
        jnp.arange(half_dim, dtype=jnp.float32) * (-2.0 * math.log(10000.0) / HEAD_DIM)
    )
    scaled = positions.astype(jnp.float32) * (TRAIN_CTX / MAX_POS)
    angle = scaled[:, None] * inverse[None, :]
    return (jnp.cos(angle)[:, None, :], jnp.sin(angle)[:, None, :])


def rotate(vectors, cosine, sine):
    half_dim = vectors.shape[-1] // 2
    first = vectors[..., :half_dim]
    second = vectors[..., half_dim:]
    return jnp.concatenate(
        [first * cosine - second * sine, second * cosine + first * sine], axis=-1
    )


def project_back(features, low_grads):
    block_width = min(features.shape[1], 512)
    block_count = features.shape[1] // block_width

    def one_block(number):
        section = lax.dynamic_slice_in_dim(features, number * block_width, block_width, 1).astype(
            jnp.float32
        )
        return lax.dot_general(
            section, low_grads, (((0,), (0,)), ((), ())), precision=lax.Precision.HIGHEST
        )

    blocks = lax.map(one_block, jnp.arange(block_count))
    return blocks.reshape(features.shape[1], low_grads.shape[1])


def local(
    hidden_states, w_query, w_key, w_value, a_query, a_value, b_query, b_value, positions, out_grad
):
    rows_here = hidden_states.shape[0]
    columns = w_query.shape[1]
    heads_here = columns // HEAD_DIM
    rank_cols = a_query.shape[1]
    scale = 1.0 / math.sqrt(HEAD_DIM)
    shard_count = lax.axis_size("ctx")
    total_tokens = rows_here * shard_count
    group_len = total_tokens // 4
    reach = (group_len // 2 % rows_here + group_len - 1) // rows_here
    full_states = lax.all_gather(hidden_states, ("head", "sub"), axis=1, tiled=True)
    pieces = (
        lax.all_gather(w_query, "ctx", axis=0, tiled=True),
        lax.all_gather(w_key, "ctx", axis=0, tiled=True),
        lax.all_gather(w_value, "ctx", axis=0, tiled=True),
    )
    base_q, base_k, base_v = tuple(
        (
            jnp.dot(full_states, weights_piece, preferred_element_type=jnp.float32)
            for weights_piece in pieces
        )
    )
    low_q = jnp.dot(full_states, a_query, preferred_element_type=jnp.float32).astype(jnp.bfloat16)
    low_v = jnp.dot(full_states, a_value, preferred_element_type=jnp.float32).astype(jnp.bfloat16)
    cosine, sine = rope_tables(positions)
    pre_q = base_q + 2.0 * jnp.dot(low_q, b_query, preferred_element_type=jnp.float32)
    queries = rotate(pre_q.reshape(rows_here, heads_here, HEAD_DIM), cosine, sine).astype(
        jnp.bfloat16
    )
    keyed = rotate(base_k.reshape(rows_here, heads_here, HEAD_DIM), cosine, sine).astype(
        jnp.bfloat16
    )
    valued = (base_v + 2.0 * jnp.dot(low_v, b_value, preferred_element_type=jnp.float32)).astype(
        jnp.bfloat16
    )
    valued = valued.reshape(rows_here, heads_here, HEAD_DIM)
    current = jnp.stack([keyed, valued])
    collected = [current]
    for level in range(reach):
        current = passed_along(current, "ctx", 1)
        collected.append(current)
    key_rows = jnp.concatenate([block[0] for block in collected], axis=0)
    value_rows = jnp.concatenate([block[1] for block in collected], axis=0)
    shard_id = lax.axis_index("ctx")
    head_ids = lax.axis_index(("head", "sub")) * heads_here + jnp.arange(heads_here)
    amount = jnp.where(head_ids >= HEADS // 2, group_len // 2, 0).astype(jnp.int32)
    query_pos = shard_id * rows_here + jnp.arange(rows_here, dtype=jnp.int32)
    block_ids = jnp.arange(reach + 1, dtype=jnp.int32)
    source_shard = (shard_id - block_ids) % shard_count
    key_pos = (
        source_shard[:, None] * rows_here + jnp.arange(rows_here, dtype=jnp.int32)[None, :]
    ).reshape(-1)
    query_num = (query_pos[None, :] - amount[:, None]) % total_tokens
    key_num = (key_pos[None, :] - amount[:, None]) % total_tokens
    same_group = key_num[:, None, :] // group_len == query_num[:, :, None] // group_len
    visible = same_group & (key_num[:, None, :] <= query_num[:, :, None])
    scores = (
        jnp.einsum("qhd,khd->hqk", queries, key_rows, preferred_element_type=jnp.float32) * scale
    )
    scores = jnp.where(visible, scores, -jnp.inf)
    highest = jnp.max(scores, axis=-1, keepdims=True)
    expo = jnp.where(visible, jnp.exp(scores - highest), 0.0)
    probs = expo / jnp.sum(expo, axis=-1, keepdims=True)
    probs_b = probs.astype(jnp.bfloat16)
    attended = jnp.einsum("hqk,khd->qhd", probs_b, value_rows, preferred_element_type=jnp.float32)
    attn_out = attended.astype(jnp.bfloat16)
    grads = out_grad.reshape(rows_here, heads_here, HEAD_DIM)
    dprob = jnp.einsum("qhd,khd->hqk", grads, value_rows, preferred_element_type=jnp.float32)
    delta = jnp.sum(grads.astype(jnp.float32) * attn_out.astype(jnp.float32), axis=-1)
    dscore = probs * (dprob - delta.T[:, :, None])
    dscore_b = (dscore * scale).astype(jnp.bfloat16)
    dquery = jnp.einsum("hqk,khd->qhd", dscore_b, key_rows, preferred_element_type=jnp.float32)
    dvalue = jnp.einsum("hqk,qhd->khd", probs_b, grads, preferred_element_type=jnp.float32)
    value_blocks = dvalue.reshape(reach + 1, rows_here, columns)
    carried = value_blocks[reach]
    for level in range(reach, 0, -1):
        carried = passed_along(carried, "ctx", -1) + value_blocks[level - 1]
    dv_local = carried.astype(jnp.bfloat16)
    dq_local = rotate(dquery, cosine, -sine).astype(jnp.bfloat16).reshape(rows_here, columns)
    grad_bq = 2.0 * jnp.dot(low_q.T, dq_local, preferred_element_type=jnp.float32)
    grad_bv = 2.0 * jnp.dot(low_v.T, dv_local, preferred_element_type=jnp.float32)
    low_grads = jnp.concatenate(
        [
            2.0 * jnp.dot(dq_local, b_query.T, preferred_element_type=jnp.float32),
            2.0 * jnp.dot(dv_local, b_value.T, preferred_element_type=jnp.float32),
        ],
        axis=1,
    )
    grad_down = lax.psum(project_back(full_states, low_grads), ("ctx", "head", "sub"))
    grad_bq, grad_bv = lax.psum((grad_bq, grad_bv), "ctx")
    return (
        attn_out.reshape(rows_here, columns),
        grad_down[:, :rank_cols],
        grad_bq,
        grad_down[:, rank_cols:],
        grad_bv,
    )


def solution(mesh):
    in_specs = (
        P(("rep", "ctx"), ("head", "sub")),
        P("ctx", ("head", "sub")),
        P("ctx", ("head", "sub")),
        P("ctx", ("head", "sub")),
        P(),
        P(),
        P(None, ("head", "sub")),
        P(None, ("head", "sub")),
        P(("rep", "ctx")),
        P(("rep", "ctx"), ("head", "sub")),
    )
    out_specs = (
        P(("rep", "ctx"), ("head", "sub")),
        P(None, "rep"),
        P("rep", ("head", "sub")),
        P(None, "rep"),
        P("rep", ("head", "sub")),
    )
    return jax.shard_map(local, mesh=mesh, in_specs=in_specs, out_specs=out_specs, check_vma=False)
```

profile of v0, /device:TPU:0, one launch (start us, length us, event | category | flops | bytes accessed | tf_op | source)
XLA Modules:
  0.0 444.1 jit_solution(10380813642152723503)
XLA Ops:
  7.2 0.7 all-gather.5.cloned.1.call-update
  8.0 0.7 all-gather.9.cloned.1.call-update
  8.7 0.7 all-gather.11.cloned.1.call-update
  9.5 0.5 all-gather.7.cloned.1.call-update
  10.2 1.3 fusion.23
  11.5 23.4 %all-gather.5.cloned.1.call-done = bf16[256,4096]{1,0:T(8,128)(2,1)} async-done(((bf16[256,1024]{1,0:T(8,128)(2,1)}), bf16[256,4096]{1,0:T(8,128)(2,1)}) %all-gather.5.cloned.1.call-update) | async-done | bytes 2097168 | tf_op jit(solution)/shard_map/all_gather | solution.py:66
  34.9 2.4 convolution_convert_fusion.1
  37.3 0.7 convolution_convert_fusion.2
  38.0 79.3 %all-gather.9.cloned.1.call-done = bf16[4096,512]{1,0:T(8,128)(2,1)} async-done(((bf16[1024,512]{1,0:T(8,128)(2,1)}), bf16[4096,512]{1,0:T(8,128)(2,1)}) %all-gather.9.cloned.1.call-update) | async-done | bytes 4194320 | tf_op jit(solution)/shard_map/all_gather | solution.py:69
  117.2 3.4 fusion.50
  120.9 77.2 %all-gather.11.cloned.1.call-done = bf16[4096,512]{1,0:T(8,128)(2,1)} async-done(((bf16[1024,512]{1,0:T(8,128)(2,1)}), bf16[4096,512]{1,0:T(8,128)(2,1)}) %all-gather.11.cloned.1.call-update) | async-done | bytes 4194320 | tf_op jit(solution)/shard_map/all_gather | solution.py:68
  198.1 3.4 fusion.51
  201.5 1.1 fusion.9
  202.6 1.2 reshape.369
  203.8 74.9 %all-gather.7.cloned.1.call-done = bf16[4096,512]{1,0:T(8,128)(2,1)} async-done(((bf16[1024,512]{1,0:T(8,128)(2,1)}), bf16[4096,512]{1,0:T(8,128)(2,1)}) %all-gather.7.cloned.1.call-update) | async-done | bytes 4194320 | tf_op jit(solution)/shard_map/all_gather | solution.py:70
  278.8 3.4 fusion.49
  282.2 0.3 fusion.10
  282.5 0.8 stack_reshape.3
  283.2 1.0 copy.29
  284.3 0.6 fusion.45
  284.9 0.3 copy-done.2
  285.2 1.1 subtract_convert_fusion.1
  286.3 1.0 pad_maximum_fusion
  287.4 1.8 copy.34
  289.2 0.8 copy_bitcast_fusion
  290.0 12.8 %collective-permute-done = bf16[2,256,4,128]{3,1,2,0:T(8,128)(2,1)S(1)} collective-permute-done((bf16[2,256,4,128]{3,1,2,0:T(8,128)(2,1)}, bf16[2,256,4,128]{3,1,2,0:T(8,128)(2,1)S(1)}, u32[]{:S(2)}, u32[]{:S(2)}) %collective-permute-start) | collective-permute-done | bytes 524320 | tf_op jit(solution)/shard_map/ppermute | solution.py:16
  302.8 0.8 slice_bitcast_fusion
  303.6 4.7 %fusion.48 = (f32[4,256]{1,0:T(4,128)S(1)}, f32[4,256,512]{2,1,0:T(8,128)}) fusion(s32[4,256]{1,0:T(4,128)S(1)} %get-tuple-element.79, s32[4,512]{1,0:T(4,128)S(1)} %get-tuple-element.74, s32[4,256]{1,0:T(4,128)S(1)} %get-tuple-element.78, s32[4,512]{1,0:T(4,128)S(1)} %get-tuple-element.73, bf16[256,4,64]{2,0,1:T(8,128)(2,1)} %get-tuple-element.56, ...), kind=kOutput, calls=%fused_computation.106 | convolution fusion | flops 142082560 | bytes 2912256 | tf_op jit(solution)/shard_map/sub | solution.py:117
  308.4 3.1 convolution_bitcast_fusion.1
  311.5 1.3 multiply_reduce_fusion
  312.9 2.6 fusion.7
  315.5 2.2 fusion.44
  318.3 1.8 copy.39
  320.4 10.3 %collective-permute-done.1 = f32[256,512]{0,1:T(8,128)} collective-permute-done((f32[256,512]{0,1:T(8,128)}, f32[256,512]{0,1:T(8,128)}, u32[]{:S(2)}, u32[]{:S(2)}) %collective-permute-start.1) | collective-permute-done | bytes 524320 | tf_op jit(solution)/shard_map/ppermute | solution.py:16
  330.7 1.1 fusion.20
  332.0 13.4 %while.10 = (s32[]{:T(128)}, f32[8,512,16]{1,0,2:T(8,128)S(1)}, s32[8]{0:T(128)S(1)}, bf16[256,4096]{1,0:T(8,128)(2,1)S(1)}, f32[256,16]{0,1:T(8,128)S(1)}, /*index=5*/s32[]{:T(128)}, s32[1]{0:T(128)}, s32[]{:T(128)}, s32[]{:T(128)}) while((s32[]{:T(128)}, f32[8,512,16]{1,0,2:T(8,128)S(1)}, s32[8]{0:T(128)S(1)}, ...), condition=%wide.region_4.5_spmd, body=%wide.region_3.4_spmd.sunk | while | flops 25165828 | bytes 442535 | solution.py:50
  332.0 0.6 dynamic_slice.12
  333.6 0.6 dynamic_slice.12
  335.3 0.6 dynamic_slice.12
  337.0 0.6 dynamic_slice.12
  338.7 0.6 dynamic_slice.12
  340.4 0.6 dynamic_slice.12
  342.0 0.6 dynamic_slice.12
  343.7 0.6 dynamic_slice.12
  345.4 0.9 copy.53
  346.4 18.4 %all-reduce = (f32[8,512]{1,0:T(8,128)}, f32[8,512]{1,0:T(8,128)}) all-reduce(f32[8,512]{1,0:T(8,128)S(1)} %convolution_multiply_fusion.3, f32[8,512]{1,0:T(8,128)S(1)} %convolution_multiply_fusion.2), channel_id=1, replica_groups=mesh['rep'=2,'ctx'=4,'head'=2,'sub'=2] {'ctx'}, use_global_device_ids=true, to_apply=%region_6.7 | all-reduce | flops 8192 | bytes 65536 | tf_op jit(solution)/shard_map/psum | solution.py:145
  364.8 71.1 %all-reduce.3.cloned.1.call-done = f32[4096,16]{0,1:T(8,128)} async-done(((f32[4096,16]{0,1:T(8,128)}), f32[4096,16]{0,1:T(8,128)}) %all-reduce.3.cloned.1.call-update) | async-done | bytes 262160 | tf_op jit(solution)/shard_map/psum | solution.py:144
  435.9 1.7 fusion.47
  (81 shorter events, 5.2 us)
Async XLA Ops:
  7.2 27.7 %copy-start = (bf16[4096,8]{0,1:T(8,128)(2,1)S(1)}, bf16[4096,8]{0,1:T(8,128)(2,1)}, u32[]{:S(2)}) copy-start(bf16[4096,8]{0,1:T(8,128)(2,1)} %param.16) | copy-start | bytes 196612
  7.2 2.9 copy-start.13
  7.2 27.7 %all-gather.5.cloned.1.call-start = ((), (), s32[]{:S(2)}) async-start(), calls=%async_computation | async-start | bytes 2621440 | tf_op jit(solution)/shard_map/all_gather | solution.py:66
  7.9 109.3 %all-gather.9.cloned.1.call-start = ((), (), s32[]{:S(2)}) async-start(), calls=%async_computation.2 | async-start | bytes 5242880 | tf_op jit(solution)/shard_map/all_gather | solution.py:69
  8.7 28.6 %copy-start.10 = (bf16[4096,8]{0,1:T(8,128)(2,1)S(1)}, bf16[4096,8]{0,1:T(8,128)(2,1)}, u32[]{:S(2)}) copy-start(bf16[4096,8]{0,1:T(8,128)(2,1)} %param.17) | copy-start | bytes 196612
  8.7 189.4 %all-gather.11.cloned.1.call-start = ((), (), s32[]{:S(2)}) async-start(), calls=%async_computation.3 | async-start | bytes 5242880 | tf_op jit(solution)/shard_map/all_gather | solution.py:68
  9.4 269.3 %all-gather.7.cloned.1.call-start = ((), (), s32[]{:S(2)}) async-start(), calls=%async_computation.1 | async-start | bytes 5242880 | tf_op jit(solution)/shard_map/all_gather | solution.py:70
  10.0 425.9 %all-reduce.3.cloned.1.call-start = ((), (), s32[]{:S(2)}) async-start(), calls=%async_computation.4 | async-start | bytes 524288 | tf_op jit(solution)/shard_map/psum | solution.py:144
  34.9 2.4 copy-start.1
  120.9 80.7 %copy-start.11 = (bf16[8,512]{1,0:T(8,128)(2,1)S(1)}, bf16[8,512]{1,0:T(8,128)(2,1)}, u32[]{:S(2)}) copy-start(bf16[8,512]{1,0:T(8,128)(2,1)} %param.18) | copy-start | bytes 24580
  203.8 78.4 %copy-start.12 = (bf16[8,512]{1,0:T(8,128)(2,1)S(1)}, bf16[8,512]{1,0:T(8,128)(2,1)}, u32[]{:S(2)}) copy-start(bf16[8,512]{1,0:T(8,128)(2,1)} %param.19) | copy-start | bytes 24580
  284.2 0.9 copy-start.2
  284.2 1.0 copy-start.5
  287.3 15.5 %collective-permute-start = (bf16[2,256,4,128]{3,1,2,0:T(8,128)(2,1)}, bf16[2,256,4,128]{3,1,2,0:T(8,128)(2,1)S(1)}, u32[]{:S(2)}, u32[]{:S(2)}) collective-permute-start(bf16[2,256,4,128]{3,1,2,0:T(8,128)(2,1)} %pad_maximum_fusion), channel_id=1, source_target_pairs={{12,0},{0,4},{4,8},{8,12},{13,1},{1,5},{5,9},{9,13},{14,2},{2,6},{... | collective-permute-start | bytes 1572872 | tf_op jit(solution)/shard_map/ppermute | solution.py:16
  303.6 4.8 %copy-start.7 = (bf16[256,512]{0,1:T(8,128)(2,1)S(1)}, bf16[256,512]{0,1:T(8,128)(2,1)}, u32[]{:S(2)}) copy-start(bf16[256,512]{0,1:T(8,128)(2,1)} %copy.34) | copy-start | bytes 786436
  308.4 3.1 copy-start.8
  308.4 3.1 copy-start.9
  308.4 3.1 copy-start.14
  315.5 2.2 copy-start.3
  315.5 2.2 copy-start.4
  317.7 13.0 %collective-permute-start.1 = (f32[256,512]{0,1:T(8,128)}, f32[256,512]{0,1:T(8,128)}, u32[]{:S(2)}, u32[]{:S(2)}) collective-permute-start(f32[256,512]{0,1:T(8,128)} %bitcast.14), channel_id=1, source_target_pairs={{4,0},{8,4},{12,8},{0,12},{5,1},{9,5},{13,9},{1,13},{6,2},{10,6},{... | collective-permute-start | bytes 1572872 | tf_op jit(solution)/shard_map/ppermute | solution.py:16
  318.0 14.0 %copy-start.6 = (f32[8,512,16]{1,0,2:T(8,128)S(1)}, f32[8,512,16]{1,0,2:T(8,128)}, u32[]{:S(2)}) copy-start(f32[8,512,16]{1,0,2:T(8,128)} %custom-call) | copy-start | bytes 786436
Sparse Core Ops, SparseCore 0:
  9.6 25.2 all-gather.4
  36.5 80.7 all-gather.8
  118.8 79.2 all-gather.10
  199.5 79.2 all-gather.6
  346.4 89.4 all-reduce.2
where the time goes:
time: 445 us; the launch traced here: 444 us
  waiting for transfers between devices  352 us (79%)
  matrix products  28.9 us (6%)
  local copies, waits for them, and re-layouts  20.4 us (5%)
  blocking collectives  18.4 us (4%)
  between operations  14.1 us (3%)
  loops' own time  5.47 us (1%)
  other arithmetic  5.13 us (1%)
    all_gather x1, waiting for transfers between devices, local(): lax.all_gather(w_key, 'ctx', axis=0, tiled=True)  79.3 us
    all_gather x1, waiting for transfers between devices, local(): lax.all_gather(w_query, 'ctx', axis=0, tiled=True)  77.2 us
    all_gather x1, waiting for transfers between devices, local(): lax.all_gather(w_value, 'ctx', axis=0, tiled=True)  74.9 us
    psum x1, waiting for transfers between devices, local(): lax.psum(project_back(full_states, low_grads), ('ctx', 'head', 'sub'))  71.1 us
    all_gather x1, waiting for transfers between devices, local(): lax.all_gather(hidden_states, ('head', 'sub'), axis=1, tiled=True)  23.4 us
    ppermute x2, waiting for transfers between devices, passed_along(): return lax.ppermute(block, axis, route)  23.1 us
    psum x1, blocking collectives, local(): grad_bq, grad_bv = lax.psum((grad_bq, grad_bv), 'ctx')  18.4 us
    dot_general x3, matrix products, local(): jnp.dot(full_states, weights_piece, preferred_element_type=jnp.float32)  10.3 us
  transfers between devices with their start and end apart: 7, of which 7 were waited for; matrix products, arithmetic and copies ran while one was open for 4% of the time, Pallas kernels for 0%

commit v1 on v0

--- a/solution.py
+++ b/solution.py
@@ -141,7 +141,9 @@
         ],
         axis=1,
     )
-    grad_down = lax.psum(project_back(full_states, low_grads), ("ctx", "head", "sub"))
+    x = project_back(full_states, low_grads)
+    parts = lax.all_gather(x, ("ctx", "head", "sub"))
+    grad_down = jnp.sum(parts, axis=0)
     grad_bq, grad_bv = lax.psum((grad_bq, grad_bv), "ctx")
     return (
         attn_out.reshape(rows_here, columns),

time: 445 us -> 422 us (0.948)
  waiting for transfers between devices: 352 us -> 315 us
  local copies, waits for them, and re-layouts: 20.4 us -> 30.7 us
    psum x1 -> x0, waiting for transfers between devices: 71.1 us -> none  [local(): lax.psum(project_back(full_states, low_grads), ('ctx', 'head', 'sub'))]
    all_gather x0 -> x1, waiting for transfers between devices: none -> 30.5 us  [local(): parts = lax.all_gather(x, ('ctx', 'head', 'sub'))]
    dynamic_update_slice x16, local copies, waits for them, and re-layouts: 1.47 us -> 14.3 us  [project_back(): blocks = lax.map(one_block, jnp.arange(block_count))]
where the time goes in v1:
time: 422 us; the launch traced here: 421 us
  waiting for transfers between devices  315 us (75%)
  local copies, waits for them, and re-layouts  30.7 us (7%)
  matrix products  29.3 us (7%)
  blocking collectives  18.9 us (4%)
  between operations  14.1 us (3%)
  other arithmetic  7.52 us (2%)
  loops' own time  5.32 us (1%)
    all_gather x1, waiting for transfers between devices, local(): lax.all_gather(w_key, 'ctx', axis=0, tiled=True)  79.3 us
    all_gather x1, waiting for transfers between devices, local(): lax.all_gather(w_query, 'ctx', axis=0, tiled=True)  77.2 us
    all_gather x1, waiting for transfers between devices, local(): lax.all_gather(w_value, 'ctx', axis=0, tiled=True)  74.9 us
    all_gather x1, waiting for transfers between devices, local(): parts = lax.all_gather(x, ('ctx', 'head', 'sub'))  30.5 us
    ppermute x2, waiting for transfers between devices, passed_along(): return lax.ppermute(block, axis, route)  27.5 us
    all_gather x1, waiting for transfers between devices, local(): lax.all_gather(hidden_states, ('head', 'sub'), axis=1, tiled=True)  23.4 us
    psum x1, blocking collectives, local(): grad_bq, grad_bv = lax.psum((grad_bq, grad_bv), 'ctx')  18.9 us
    dynamic_update_slice x16, local copies, waits for them, and re-layouts, project_back(): blocks = lax.map(one_block, jnp.arange(block_count))  14.3 us
  transfers between devices with their start and end apart: 7, of which 7 were waited for; matrix products, arithmetic and copies ran while one was open for 4% of the time, Pallas kernels for 0%

profile of v1, /device:TPU:0, one launch (start us, length us, event | category | flops | bytes accessed | tf_op | source)
XLA Modules:
  0.0 421.3 jit_solution(10711146232651518942)
XLA Ops:
  7.2 0.7 all-gather.6.cloned.1.call-update
  8.0 0.7 all-gather.10.cloned.1.call-update
  8.7 0.7 all-gather.12.cloned.1.call-update
  10.2 1.3 fusion.23
  11.5 23.4 %all-gather.6.cloned.1.call-done = bf16[256,4096]{1,0:T(8,128)(2,1)} async-done(((bf16[256,1024]{1,0:T(8,128)(2,1)}), bf16[256,4096]{1,0:T(8,128)(2,1)}) %all-gather.6.cloned.1.call-update) | async-done | bytes 2097168 | tf_op jit(solution)/shard_map/all_gather | solution.py:66
  34.9 2.4 convolution_convert_fusion.1
  37.3 0.7 convolution_convert_fusion.2
  38.0 79.3 %all-gather.10.cloned.1.call-done = bf16[4096,512]{1,0:T(8,128)(2,1)} async-done(((bf16[1024,512]{1,0:T(8,128)(2,1)}), bf16[4096,512]{1,0:T(8,128)(2,1)}) %all-gather.10.cloned.1.call-update) | async-done | bytes 4194320 | tf_op jit(solution)/shard_map/all_gather | solution.py:69
  117.2 3.4 fusion.50
  120.9 77.2 %all-gather.12.cloned.1.call-done = bf16[4096,512]{1,0:T(8,128)(2,1)} async-done(((bf16[1024,512]{1,0:T(8,128)(2,1)}), bf16[4096,512]{1,0:T(8,128)(2,1)}) %all-gather.12.cloned.1.call-update) | async-done | bytes 4194320 | tf_op jit(solution)/shard_map/all_gather | solution.py:68
  198.1 3.4 fusion.51
  201.5 1.1 fusion.9
  202.6 1.2 reshape.366
  203.8 74.9 %all-gather.8.cloned.1.call-done = bf16[4096,512]{1,0:T(8,128)(2,1)} async-done(((bf16[1024,512]{1,0:T(8,128)(2,1)}), bf16[4096,512]{1,0:T(8,128)(2,1)}) %all-gather.8.cloned.1.call-update) | async-done | bytes 4194320 | tf_op jit(solution)/shard_map/all_gather | solution.py:70
  278.7 3.4 fusion.49
  282.5 0.8 stack_reshape.3
  283.2 1.0 copy.41
  284.3 0.6 fusion.45
  285.2 1.1 subtract_convert_fusion.1
  286.3 1.0 pad_maximum_fusion
  287.7 15.2 %collective-permute-done = bf16[2,256,4,128]{3,1,2,0:T(8,128)(2,1)} collective-permute-done((bf16[2,256,4,128]{3,1,2,0:T(8,128)(2,1)}, bf16[2,256,4,128]{3,1,2,0:T(8,128)(2,1)}, u32[]{:S(2)}, u32[]{:S(2)}) %collective-permute-start) | collective-permute-done | bytes 524320 | tf_op jit(solution)/shard_map/ppermute | solution.py:16
  302.9 1.8 slice_bitcast_fusion
  304.7 4.7 %fusion.48 = (f32[4,256]{1,0:T(4,128)S(1)}, f32[4,256,512]{2,1,0:T(8,128)}) fusion(s32[4,256]{1,0:T(4,128)S(1)} %get-tuple-element.84, s32[4,512]{1,0:T(4,128)S(1)} %get-tuple-element.79, s32[4,256]{1,0:T(4,128)S(1)} %get-tuple-element.83, s32[4,512]{1,0:T(4,128)S(1)} %get-tuple-element.78, bf16[256,4,64]{2,0,1:T(8,128)(2,1)} %get-tuple-element.61, ...), kind=kOutput, calls=%fused_computation.106 | convolution fusion | flops 142082560 | bytes 2912256 | tf_op jit(solution)/shard_map/sub | solution.py:117
  309.4 3.1 convolution_bitcast_fusion.1
  312.6 1.6 multiply_reduce_fusion
  314.2 2.7 fusion.7
  316.9 2.2 fusion.44
  319.8 12.3 %collective-permute-done.1 = f32[256,512]{0,1:T(8,128)} collective-permute-done((f32[256,512]{0,1:T(8,128)}, f32[256,512]{0,1:T(8,128)}, u32[]{:S(2)}, u32[]{:S(2)}) %collective-permute-start.1) | collective-permute-done | bytes 524320 | tf_op jit(solution)/shard_map/ppermute | solution.py:16
  332.1 1.1 fusion.20
  333.3 26.1 %while.10 = (s32[]{:T(128)}, f32[8,512,16]{1,0,2:T(8,128)}, s32[8]{0:T(128)S(1)}, bf16[256,4096]{1,0:T(8,128)(2,1)S(1)}, f32[256,16]{0,1:T(8,128)S(1)}, /*index=5*/s32[]{:T(128)}, s32[1]{0:T(128)}, s32[]{:T(128)}, s32[]{:T(128)}) while((s32[]{:T(128)}, f32[8,512,16]{1,0,2:T(8,128)}, s32[8]{0:T(128)S(1)}, bf16[256,4096]{1,0:T(8,128)(2,1)S(1)}, ...), condition=%wide.region_4.5_spmd, body=%wide.region_3.4_spmd.sunk | while | flops 25165828 | bytes 442535 | solution.py:50
  333.3 0.6 dynamic_slice.12
  334.8 1.8 dynamic_update_slice.5
  338.1 1.8 dynamic_update_slice.5
  339.9 0.6 dynamic_slice.12
  341.4 1.8 dynamic_update_slice.5
  344.6 1.8 dynamic_update_slice.5
  346.4 0.6 dynamic_slice.12
  347.9 1.8 dynamic_update_slice.5
  349.6 0.6 dynamic_slice.12
  351.1 1.8 dynamic_update_slice.5
  354.4 1.8 dynamic_update_slice.5
  357.6 1.8 dynamic_update_slice.5
  359.4 1.7 all_gather_reshape.3
  361.1 0.8 copy.53
  362.3 18.9 %all-reduce = (f32[8,512]{1,0:T(8,128)}, f32[8,512]{1,0:T(8,128)}) all-reduce(f32[8,512]{1,0:T(8,128)S(1)} %convolution_multiply_fusion.3, f32[8,512]{1,0:T(8,128)S(1)} %convolution_multiply_fusion.2), channel_id=1, replica_groups=mesh['rep'=2,'ctx'=4,'head'=2,'sub'=2] {'ctx'}, use_global_device_ids=true, to_apply=%region_6.7 | all-reduce | flops 8192 | bytes 65536 | tf_op jit(solution)/shard_map/psum | solution.py:147
  381.2 30.5 %all-gather.14.cloned.1.call-done = f32[16,4096,16]{1,2,0:T(8,128)} async-done(((f32[1,4096,16]{1,2,0:T(8,128)}), f32[16,4096,16]{1,2,0:T(8,128)}) %all-gather.14.cloned.1.call-update) | async-done | bytes 4194320 | tf_op jit(solution)/shard_map/all_gather | solution.py:145
  411.7 2.4 reduce_sum.29
  414.1 0.7 fusion.47
  (84 shorter events, 7.7 us)
Async XLA Ops:
  7.2 27.7 %copy-start = (bf16[4096,8]{0,1:T(8,128)(2,1)S(1)}, bf16[4096,8]{0,1:T(8,128)(2,1)}, u32[]{:S(2)}) copy-start(bf16[4096,8]{0,1:T(8,128)(2,1)} %param.16) | copy-start | bytes 196612
  7.2 2.9 copy-start.14
  7.2 27.7 %all-gather.6.cloned.1.call-start = ((), (), s32[]{:S(2)}) async-start(), calls=%async_computation | async-start | bytes 2621440 | tf_op jit(solution)/shard_map/all_gather | solution.py:66
  7.9 109.3 %all-gather.10.cloned.1.call-start = ((), (), s32[]{:S(2)}) async-start(), calls=%async_computation.2 | async-start | bytes 5242880 | tf_op jit(solution)/shard_map/all_gather | solution.py:69
  8.7 28.6 %copy-start.11 = (bf16[4096,8]{0,1:T(8,128)(2,1)S(1)}, bf16[4096,8]{0,1:T(8,128)(2,1)}, u32[]{:S(2)}) copy-start(bf16[4096,8]{0,1:T(8,128)(2,1)} %param.17) | copy-start | bytes 196612
  8.7 189.4 %all-gather.12.cloned.1.call-start = ((), (), s32[]{:S(2)}) async-start(), calls=%async_computation.3 | async-start | bytes 5242880 | tf_op jit(solution)/shard_map/all_gather | solution.py:68
  9.4 269.3 %all-gather.8.cloned.1.call-start = ((), (), s32[]{:S(2)}) async-start(), calls=%async_computation.1 | async-start | bytes 5242880 | tf_op jit(solution)/shard_map/all_gather | solution.py:70
  10.0 401.7 %all-gather.14.cloned.1.call-start = ((), (), s32[]{:S(2)}) async-start(), calls=%async_computation.4 | async-start | bytes 4456448 | tf_op jit(solution)/shard_map/all_gather | solution.py:145
  34.9 2.4 copy-start.1
  120.9 80.6 %copy-start.12 = (bf16[8,512]{1,0:T(8,128)(2,1)S(1)}, bf16[8,512]{1,0:T(8,128)(2,1)}, u32[]{:S(2)}) copy-start(bf16[8,512]{1,0:T(8,128)(2,1)} %param.18) | copy-start | bytes 24580
  203.8 78.4 %copy-start.13 = (bf16[8,512]{1,0:T(8,128)(2,1)S(1)}, bf16[8,512]{1,0:T(8,128)(2,1)}, u32[]{:S(2)}) copy-start(bf16[8,512]{1,0:T(8,128)(2,1)} %param.19) | copy-start | bytes 24580
  284.2 0.9 copy-start.2
  284.2 1.0 copy-start.5
  285.2 2.1 copy-start.6
  287.3 15.6 %collective-permute-start = (bf16[2,256,4,128]{3,1,2,0:T(8,128)(2,1)}, bf16[2,256,4,128]{3,1,2,0:T(8,128)(2,1)}, u32[]{:S(2)}, u32[]{:S(2)}) collective-permute-start(bf16[2,256,4,128]{3,1,2,0:T(8,128)(2,1)} %pad_maximum_fusion), channel_id=1, source_target_pairs={{12,0},{0,4},{4,8},{8,12},{13,1},{1,5},{5,9},{9,13},{14,2},{2,6},{... | collective-permute-start | bytes 1572872 | tf_op jit(solution)/shard_map/ppermute | solution.py:16
  287.5 21.9 %copy-start.7 = (bf16[256,512]{0,1:T(8,128)(2,1)}, bf16[256,512]{0,1:T(8,128)(2,1)S(1)}, u32[]{:S(2)}) copy-start(bf16[256,512]{0,1:T(8,128)(2,1)S(1)} %copy.46) | copy-start | bytes 786436
  287.6 24.9 %copy-start.8 = (bf16[256,4,128]{2,0,1:T(8,128)(2,1)}, bf16[256,4,128]{2,0,1:T(8,128)(2,1)S(1)}, u32[]{:S(2)}) copy-start(bf16[256,4,128]{2,0,1:T(8,128)(2,1)S(1)} %copy_bitcast_fusion) | copy-start | bytes 786436
  304.7 4.7 %copy-start.9 = (bf16[256,4,128]{2,0,1:T(8,128)(2,1)}, bf16[256,4,128]{2,0,1:T(8,128)(2,1)S(1)}, u32[]{:S(2)}) copy-start(bf16[256,4,128]{2,0,1:T(8,128)(2,1)S(1)} %get-tuple-element.68) | copy-start | bytes 786436
  309.4 3.2 copy-start.10
  309.4 3.1 copy-start.15
  316.9 2.2 copy-start.3
  316.9 2.2 copy-start.4
  319.1 13.0 %collective-permute-start.1 = (f32[256,512]{0,1:T(8,128)}, f32[256,512]{0,1:T(8,128)}, u32[]{:S(2)}, u32[]{:S(2)}) collective-permute-start(f32[256,512]{0,1:T(8,128)} %bitcast.14), channel_id=1, source_target_pairs={{4,0},{8,4},{12,8},{0,12},{5,1},{9,5},{13,9},{1,13},{6,2},{10,6},{... | collective-permute-start | bytes 1572872 | tf_op jit(solution)/shard_map/ppermute | solution.py:16
Sparse Core Ops, SparseCore 0:
  9.6 25.2 all-gather.5
  36.5 80.7 all-gather.9
  118.8 79.2 all-gather.11
  199.5 79.2 all-gather.7
  361.3 50.3 all-gather.13
